TPU v7x, 512 devices: a whole 4x4x16 slice. The times are simulated.
512 devices in a mesh: row: 16 (over z_lo, y), col: 32 (over x, z_hi, core).
Axes of the slice: x: 4, y: 4, z: 16 (z_hi: 4, z_lo: 4; z = z_hi * 4 + z_lo), core: 2. Of those that a mesh axis runs over, the one named last changes fastest.
Arguments:
- tiles: bfloat16 [16, 32, 32, 128, 128], P('row', 'col'), may hold values from -0.5 to 0.5
- tile_slots: int32 [16, 32, 32], P('row', 'col'), may hold values from 0 to 191, as said below
- tile_counts: int32 [16, 32], P('row', 'col'), may hold values from 8 to 32, as said below
- user_degree: int32 [32768], P('row'), may hold values from 1 to 64
- item_degree: int32 [49152], P('col'), may hold values from 1 to 64
- start_panel: float32 [64, 49152], P(None, ('col', 'row')), may hold values from -6 to 6
Outputs:
- left_panel: float32 [64, 32768], P(None, ('row', 'col'))
- right_panel: float32 [64, 49152], P(None, ('col', 'row'))
- left_factors: float32 [3, 64, 64], replicated
- right_factors: float32 [3, 64, 64], replicated
Inputs may be any that keep to these rules, and one draw needn't show every extreme that they name: `tile_slots`: within one grid cell the 32 slot numbers are distinct; slot s is local tile row s // 12 and local tile column s % 12; entries from position tile_counts on are padding. `tile_counts`: some grid cell holds 32 live tiles.
All inputs are finite; a program needn't handle non-finite values.
Results may differ from a plain program's by a relative error of at most 0.0005.
Values sent between devices are 32-bit elements; how exact they have to be, the bound alone decides.
No kernel may reach another device: no remote copies, remote signals or barrier semaphores. Data moves between devices by JAX's collectives and lax.ppermute only.
A program may use at most 64 MiB of HBM per device.

v0:
```python
import math
import jax
import jax.numpy as jnp
from jax import lax
from jax.sharding import PartitionSpec as P

STEPS = 3
HIGH = lax.Precision.HIGHEST


def gram_of(vectors):
    return jnp.einsum("bn,cn->bc", vectors, vectors, precision=HIGH)


def solve_lower(factor, vectors):
    return lax.linalg.triangular_solve(factor, vectors, left_side=True, lower=True)


def per_device(tiles, tile_slots, tile_counts, user_degree, item_degree, start_panel):
    tile_stack = tiles[0, 0].astype(jnp.float32)
    slot_list = tile_slots[0, 0]
    tile_total = tile_counts[0, 0]
    slot_count = tile_stack.shape[0]
    tile_width = tile_stack.shape[1]
    row_blocks = user_degree.shape[0] // tile_width
    col_blocks = item_degree.shape[0] // tile_width
    block_width = start_panel.shape[0]
    live_mask = jnp.arange(slot_count) < tile_total
    local_rows = slot_list // col_blocks
    local_cols = slot_list % col_blocks
    row_select = (
        (local_rows[:, None] == jnp.arange(row_blocks)[None, :]) & live_mask[:, None]
    ).astype(jnp.float32)
    col_select = (
        (local_cols[:, None] == jnp.arange(col_blocks)[None, :]) & live_mask[:, None]
    ).astype(jnp.float32)
    user_scale = lax.rsqrt(user_degree.astype(jnp.float32))
    item_scale = lax.rsqrt(item_degree.astype(jnp.float32))
    user_group = row_blocks * tile_width // lax.axis_size("col")
    item_group = col_blocks * tile_width // lax.axis_size("row")
    user_offset = lax.axis_index("col") * user_group
    item_offset = lax.axis_index("row") * item_group
    user_scale_own = lax.dynamic_slice_in_dim(user_scale, user_offset, user_group)
    item_scale_own = lax.dynamic_slice_in_dim(item_scale, item_offset, item_group)
    start_total = lax.psum(gram_of(start_panel), ("row", "col"))
    start_factor = jnp.linalg.cholesky(start_total)
    item_basis = solve_lower(start_factor, start_panel)
    user_basis = start_panel[:, :0]
    item_factor = start_factor
    user_list = []
    item_list = []
    for iteration in range(STEPS):
        scaled = item_basis * item_scale_own[None, :]
        item_full = lax.all_gather(scaled, "row", axis=1, tiled=True)
        forward_panel_blocks = item_full.reshape(block_width, col_blocks, tile_width)
        forward_chosen = jnp.take(forward_panel_blocks, local_cols, axis=1)
        forward_partial_value = jnp.einsum(
            "mrc,bmc->bmr", tile_stack, forward_chosen, precision=HIGH
        )
        forward_summed = jnp.einsum(
            "bmr,mk->bkr", forward_partial_value, row_select, precision=HIGH
        )
        forward = (
            lax.psum_scatter(
                forward_summed.reshape(block_width, row_blocks * tile_width),
                "col",
                scatter_dimension=1,
                tiled=True,
            )
            * user_scale_own[None, :]
        )
        if iteration > 0:
            forward = forward - jnp.dot(item_factor.T, user_basis, precision=HIGH)
        user_factor = jnp.linalg.cholesky(lax.psum(gram_of(forward), ("row", "col")))
        user_basis = solve_lower(user_factor, forward)
        scaled = user_basis * user_scale_own[None, :]
        user_full = lax.all_gather(scaled, "col", axis=1, tiled=True)
        panel_blocks = user_full.reshape(block_width, row_blocks, tile_width)
        chosen = jnp.take(panel_blocks, local_rows, axis=1)
        partial_value = jnp.einsum("mrc,bmr->bmc", tile_stack, chosen, precision=HIGH)
        summed = jnp.einsum("bmc,mk->bkc", partial_value, col_select, precision=HIGH)
        backward = (
            lax.psum_scatter(
                summed.reshape(block_width, col_blocks * tile_width),
                "row",
                scatter_dimension=1,
                tiled=True,
            )
            * item_scale_own[None, :]
        )
        backward = backward - jnp.dot(user_factor.T, item_basis, precision=HIGH)
        item_factor = jnp.linalg.cholesky(lax.psum(gram_of(backward), ("row", "col")))
        item_basis = solve_lower(item_factor, backward)
        user_list.append(user_factor)
        item_list.append(item_factor)
    user_total = row_blocks * tile_width * lax.axis_size("row")
    item_total = col_blocks * tile_width * lax.axis_size("col")
    return (
        math.sqrt(user_total) * user_basis,
        math.sqrt(item_total) * item_basis,
        jnp.stack(user_list),
        jnp.stack(item_list),
    )


def solution(mesh):
    in_specs = (
        P("row", "col", None, None, None),
        P("row", "col", None),
        P("row", "col"),
        P("row"),
        P("col"),
        P(None, ("col", "row")),
    )
    out_specs = (P(None, ("row", "col")), P(None, ("col", "row")), P(), P())
    return jax.shard_map(
        per_device, mesh=mesh, in_specs=in_specs, out_specs=out_specs, check_vma=False
    )
```

profile of v0, /device:TPU:1, one launch (start us, length us, event | category | flops | bytes accessed | tf_op | source)
XLA Modules:
  0.0 1727.9 jit_solution(9248479124465914468)
XLA Ops:
  9.7 111.2 %psum.49 = f32[64,64]{0,1:T(8,128)S(1)} all-reduce(f32[64,64]{0,1:T(8,128)S(1)} %fusion.153), channel_id=1, replica_groups=mesh['row'=16,'col'=32] {'row','col'}, use_global_device_ids=true, to_apply=%region_0.1 | all-reduce | flops 4096 | bytes 32768 | tf_op jit(solution)/shard_map/psum | solution.py:45
  120.9 5.8 cholesky.119
  128.1 4.9 custom-call.13
  134.1 33.8 %all-gather = f32[16,96,64]{1,2,0:T(8,128)S(1)} all-gather(f32[1,96,64]{1,2,0:T(8,128)S(1)} %multiply_bitcast_fusion.2), channel_id=1, replica_groups=mesh['row'=16,'col'=32] {'row'}, dimensions={0}, use_global_device_ids=true | all-gather | bytes 417792 | tf_op jit(solution)/shard_map/all_gather | solution.py:54
  169.1 2.2 convolution_bitcast_fusion.5
  171.3 1.1 convolution_bitcast_fusion.11
  172.4 1.4 copy.162
  174.6 110.4 %reduce-scatter.19.cloned.1.call-done = f32[64,64]{1,0:T(8,128)} async-done(((f32[2048,64]{1,0:T(8,128)}), f32[64,64]{1,0:T(8,128)}) %reduce-scatter.19.cloned.1.call-update) | async-done | bytes 16400
  286.0 101.8 %psum.50 = f32[64,64]{0,1:T(8,128)S(1)} all-reduce(f32[64,64]{0,1:T(8,128)S(1)} %fusion.81), channel_id=1, replica_groups=mesh['row'=16,'col'=32] {'row','col'}, use_global_device_ids=true, to_apply=%region_4.8 | all-reduce | flops 4096 | bytes 32768 | tf_op jit(solution)/shard_map/psum | solution.py:74
  388.0 5.8 cholesky.130
  395.1 4.9 custom-call.14
  400.4 57.0 %all_gather.19 = f32[64,2048]{0,1:T(8,128)S(1)} all-gather(f32[64,64]{0,1:T(8,128)S(1)} %copy.109), channel_id=1, replica_groups=mesh['row'=16,'col'=32] {'col'}, dimensions={1}, use_global_device_ids=true | all-gather | bytes 540672 | tf_op jit(solution)/shard_map/all_gather | solution.py:77
  459.3 1.1 convolution_bitcast_fusion.10
  460.4 1.2 copy.163
  461.6 71.2 %reduce-scatter.21.cloned.1.call-done = f32[96,64]{1,0:T(8,128)} async-done(((f32[1536,64]{1,0:T(8,128)}), f32[96,64]{1,0:T(8,128)}) %reduce-scatter.21.cloned.1.call-update) | async-done | bytes 24592
  534.8 112.8 %psum.51 = f32[64,64]{0,1:T(8,128)S(1)} all-reduce(f32[64,64]{0,1:T(8,128)S(1)} %fusion.154), channel_id=1, replica_groups=mesh['row'=16,'col'=32] {'row','col'}, use_global_device_ids=true, to_apply=%region_6.12 | all-reduce | flops 4096 | bytes 32768 | tf_op jit(solution)/shard_map/psum | solution.py:92
  647.7 5.8 cholesky.141
  654.9 4.9 custom-call.15
  660.0 36.4 %all-gather.1 = f32[16,96,64]{1,2,0:T(8,128)S(1)} all-gather(f32[1,96,64]{1,2,0:T(8,128)S(1)} %multiply_bitcast_fusion.1), channel_id=1, replica_groups=mesh['row'=16,'col'=32] {'row'}, dimensions={0}, use_global_device_ids=true | all-gather | bytes 417792 | tf_op jit(solution)/shard_map/all_gather | solution.py:54
  697.6 2.2 convolution_bitcast_fusion.3
  699.8 1.1 convolution_bitcast_fusion.9
  700.9 1.4 copy.164
  702.3 110.1 %reduce-scatter.23.cloned.1.call-done = f32[64,64]{1,0:T(8,128)} async-done(((f32[2048,64]{1,0:T(8,128)}), f32[64,64]{1,0:T(8,128)}) %reduce-scatter.23.cloned.1.call-update) | async-done | bytes 16400
  814.3 102.0 %psum.52 = f32[64,64]{0,1:T(8,128)S(1)} all-reduce(f32[64,64]{0,1:T(8,128)S(1)} %fusion.155), channel_id=1, replica_groups=mesh['row'=16,'col'=32] {'row','col'}, use_global_device_ids=true, to_apply=%region_8.14 | all-reduce | flops 4096 | bytes 32768 | tf_op jit(solution)/shard_map/psum | solution.py:74
  916.4 5.8 cholesky.152
  923.6 4.9 custom-call.16
  928.9 56.4 %all_gather.21 = f32[64,2048]{0,1:T(8,128)S(1)} all-gather(f32[64,64]{0,1:T(8,128)S(1)} %copy.120), channel_id=1, replica_groups=mesh['row'=16,'col'=32] {'col'}, dimensions={1}, use_global_device_ids=true | all-gather | bytes 540672 | tf_op jit(solution)/shard_map/all_gather | solution.py:77
  987.2 1.1 convolution_bitcast_fusion.8
  988.3 1.2 copy.165
  989.6 70.9 %reduce-scatter.25.cloned.1.call-done = f32[96,64]{1,0:T(8,128)} async-done(((f32[1536,64]{1,0:T(8,128)}), f32[96,64]{1,0:T(8,128)}) %reduce-scatter.25.cloned.1.call-update) | async-done | bytes 24592
  1062.5 113.1 %psum.53 = f32[64,64]{0,1:T(8,128)S(1)} all-reduce(f32[64,64]{0,1:T(8,128)S(1)} %fusion.156), channel_id=1, replica_groups=mesh['row'=16,'col'=32] {'row','col'}, use_global_device_ids=true, to_apply=%region_10.16 | all-reduce | flops 4096 | bytes 32768 | tf_op jit(solution)/shard_map/psum | solution.py:92
  1175.6 5.8 cholesky.163
  1182.8 4.9 custom-call.17
  1188.0 36.7 %all-gather.2 = f32[16,96,64]{1,2,0:T(8,128)S(1)} all-gather(f32[1,96,64]{1,2,0:T(8,128)S(1)} %multiply_bitcast_fusion), channel_id=1, replica_groups=mesh['row'=16,'col'=32] {'row'}, dimensions={0}, use_global_device_ids=true | all-gather | bytes 417792 | tf_op jit(solution)/shard_map/all_gather | solution.py:54
  1225.9 2.2 convolution_bitcast_fusion.1
  1228.0 1.1 convolution_bitcast_fusion.7
  1229.1 1.4 copy.166
  1230.5 110.1 %reduce-scatter.27.cloned.1.call-done = f32[64,64]{1,0:T(8,128)} async-done(((f32[2048,64]{1,0:T(8,128)}), f32[64,64]{1,0:T(8,128)}) %reduce-scatter.27.cloned.1.call-update) | async-done | bytes 16400
  1342.5 101.8 %psum.54 = f32[64,64]{0,1:T(8,128)S(1)} all-reduce(f32[64,64]{0,1:T(8,128)S(1)} %fusion.157), channel_id=1, replica_groups=mesh['row'=16,'col'=32] {'row','col'}, use_global_device_ids=true, to_apply=%region_12.18 | all-reduce | flops 4096 | bytes 32768 | tf_op jit(solution)/shard_map/psum | solution.py:74
  1444.4 5.8 cholesky.174
  1451.6 4.9 custom-call.18
  1457.5 56.3 %all_gather.23 = f32[64,2048]{0,1:T(8,128)S(1)} all-gather(f32[64,64]{0,1:T(8,128)S(1)} %copy.131), channel_id=1, replica_groups=mesh['row'=16,'col'=32] {'col'}, dimensions={1}, use_global_device_ids=true | all-gather | bytes 540672 | tf_op jit(solution)/shard_map/all_gather | solution.py:77
  1515.7 1.1 convolution_bitcast_fusion.6
  1516.8 1.2 copy.167
  1518.7 73.4 %reduce-scatter.29.cloned.1.call-done = f32[96,64]{1,0:T(8,128)} async-done(((f32[1536,64]{1,0:T(8,128)}), f32[96,64]{1,0:T(8,128)}) %reduce-scatter.29.cloned.1.call-update) | async-done | bytes 24592
  1594.0 113.0 %psum.55 = f32[64,64]{0,1:T(8,128)S(1)} all-reduce(f32[64,64]{0,1:T(8,128)S(1)} %fusion.158), channel_id=1, replica_groups=mesh['row'=16,'col'=32] {'row','col'}, use_global_device_ids=true, to_apply=%region_14.20 | all-reduce | flops 4096 | bytes 32768 | tf_op jit(solution)/shard_map/psum | solution.py:92
  1707.1 5.8 cholesky.185
  1714.3 4.9 custom-call.19
  (114 shorter events, 38.1 us)
Async XLA Ops:
  7.2 161.9 %copy-start = (bf16[1,1,32,128,128]{4,3,2,1,0:T(8,128)(2,1)S(1)}, bf16[1,1,32,128,128]{4,3,2,1,0:T(8,128)(2,1)}, u32[]{:S(2)}) copy-start(bf16[1,1,32,128,128]{4,3,2,1,0:T(8,128)(2,1)} %param.15) | copy-start | bytes 3145732
  7.2 277.8 %reduce-scatter.19.cloned.1.call-start = ((), (), s32[]{:S(2)}) async-start(), calls=%async_computation.6 | async-start | bytes 1081344
  8.0 0.7 copy-start.2
  127.5 5.6 copy-start.1
  173.7 359.1 %reduce-scatter.21.cloned.1.call-start = ((), (), s32[]{:S(2)}) async-start(), calls=%async_computation.7 | async-start | bytes 835584
  461.6 350.8 %reduce-scatter.23.cloned.1.call-start = ((), (), s32[]{:S(2)}) async-start(), calls=%async_computation.8 | async-start | bytes 1081344
  702.3 358.2 %reduce-scatter.25.cloned.1.call-start = ((), (), s32[]{:S(2)}) async-start(), calls=%async_computation.9 | async-start | bytes 835584
  989.5 351.1 %reduce-scatter.27.cloned.1.call-start = ((), (), s32[]{:S(2)}) async-start(), calls=%async_computation.10 | async-start | bytes 1081344
  1230.5 361.6 %reduce-scatter.29.cloned.1.call-start = ((), (), s32[]{:S(2)}) async-start(), calls=%async_computation.11 | async-start | bytes 835584
Sparse Core Ops, SparseCore 0:
  173.9 111.0 reduce-scatter.18
  461.7 71.0 reduce-scatter.20
  702.4 109.9 reduce-scatter.22
  989.6 70.8 reduce-scatter.24
  1230.6 109.9 reduce-scatter.26
  1518.1 73.8 reduce-scatter.28
where the time goes:
time: 1740 us; the launch traced here: 1730 us
  blocking collectives  1030 us (59%)
  waiting for transfers between devices  546 us (31%)
  other arithmetic  87.5 us (5%)
  matrix products  25.6 us (1%)
  local copies, waits for them, and re-layouts  20.4 us (1%)
    unnamed x12, waiting for transfers between devices  546 us
    psum x3, blocking collectives, per_device(): lax.psum(gram_of(backward), ('row', 'col'))  339 us
    psum x3, blocking collectives, per_device(): lax.psum(gram_of(forward), ('row', 'col'))  306 us
    all_gather x3, blocking collectives, per_device(): user_full = lax.all_gather(scaled, 'col', axis=1, tiled=True)  170 us
    psum x1, blocking collectives, per_device(): start_total = lax.psum(gram_of(start_panel), ('row', 'col'))  111 us
    all_gather x3, blocking collectives, per_device(): item_full = lax.all_gather(scaled, 'row', axis=1, tiled=True)  107 us
    another operation x8, other arithmetic, solve_lower(): lax.linalg.triangular_solve(factor, vectors, left_side=True, lower=True)  34.9 us
  transfers between devices with their start and end apart: 6, of which 6 were waited for; matrix products, arithmetic and copies ran while one was open for 0% of the time, Pallas kernels for 0%

commit v1 on v0

--- a/solution.py
+++ b/solution.py
@@ -51,7 +51,9 @@
     item_list = []
     for iteration in range(STEPS):
         scaled = item_basis * item_scale_own[None, :]
-        item_full = lax.all_gather(scaled, "row", axis=1, tiled=True)
+        item_full = jnp.concatenate(
+            lax.all_to_all(jnp.stack([scaled] * lax.axis_size("row")), "row", 0, 0), axis=1
+        )
         forward_panel_blocks = item_full.reshape(block_width, col_blocks, tile_width)
         forward_chosen = jnp.take(forward_panel_blocks, local_cols, axis=1)
         forward_partial_value = jnp.einsum(

time: 1740 us -> 1670 us (0.960)
  blocking collectives: 1030 us -> 965 us
    all_gather x3 -> x0, blocking collectives: 107 us -> none  [per_device(): item_full = lax.all_gather(scaled, 'row', axis=1, tiled=True)]
    all_to_all x0 -> x2, blocking collectives: none -> 38 us  [per_device(): lax.all_to_all(jnp.stack([scaled] * lax.axis_size('row')), 'row', 0, 0)]
  transfers between devices with their start and end apart: 6 -> 7, of which waited for: 6 -> 7; matrix products, arithmetic and copies ran while one was open for 0% -> 0% of each run, Pallas kernels for 0% -> 0%
where the time goes in v1:
time: 1670 us; the launch traced here: 1660 us
  blocking collectives  965 us (58%)
  waiting for transfers between devices  541 us (32%)
  other arithmetic  87.5 us (5%)
  matrix products  25.6 us (2%)
  local copies, waits for them, and re-layouts  21.4 us (1%)
    unnamed x12, waiting for transfers between devices  529 us
    psum x3, blocking collectives, per_device(): lax.psum(gram_of(backward), ('row', 'col'))  339 us
    psum x3, blocking collectives, per_device(): lax.psum(gram_of(forward), ('row', 'col'))  306 us
    all_gather x3, blocking collectives, per_device(): user_full = lax.all_gather(scaled, 'col', axis=1, tiled=True)  171 us
    psum x1, blocking collectives, per_device(): start_total = lax.psum(gram_of(start_panel), ('row', 'col'))  111 us
    all_to_all x2, blocking collectives, per_device(): lax.all_to_all(jnp.stack([scaled] * lax.axis_size('row')), 'row', 0, 0)  38 us
    another operation x8, other arithmetic, solve_lower(): lax.linalg.triangular_solve(factor, vectors, left_side=True, lower=True)  34.9 us
  transfers between devices with their start and end apart: 7, of which 7 were waited for; matrix products, arithmetic and copies ran while one was open for 0% of the time, Pallas kernels for 0%

profile of v1, /device:TPU:1, one launch (start us, length us, event | category | flops | bytes accessed | tf_op | source)
XLA Modules:
  0.0 1660.6 jit_solution(11717541913926504305)
XLA Ops:
  8.2 111.2 %psum.49 = f32[64,64]{0,1:T(8,128)S(1)} all-reduce(f32[64,64]{0,1:T(8,128)S(1)} %fusion.153), channel_id=1, replica_groups=mesh['row'=16,'col'=32] {'row','col'}, use_global_device_ids=true, to_apply=%region_0.1 | all-reduce | flops 4096 | bytes 32768 | tf_op jit(solution)/shard_map/psum | solution.py:45
  119.5 5.8 cholesky.119
  126.7 4.9 custom-call.13
  133.5 3.6 all-to-all-start
  138.4 12.4 all-to-all-done
  152.1 2.2 convolution_bitcast_fusion.5
  154.3 1.1 convolution_bitcast_fusion.11
  155.4 1.4 copy.133
  157.6 105.9 %reduce-scatter.19.cloned.1.call-done = f32[64,64]{1,0:T(8,128)} async-done(((f32[2048,64]{1,0:T(8,128)}), f32[64,64]{1,0:T(8,128)}) %reduce-scatter.19.cloned.1.call-update) | async-done | bytes 16400
  264.6 101.8 %psum.50 = f32[64,64]{0,1:T(8,128)S(1)} all-reduce(f32[64,64]{0,1:T(8,128)S(1)} %fusion.81), channel_id=1, replica_groups=mesh['row'=16,'col'=32] {'row','col'}, use_global_device_ids=true, to_apply=%region_4.8 | all-reduce | flops 4096 | bytes 32768 | tf_op jit(solution)/shard_map/psum | solution.py:76
  366.5 5.8 cholesky.130
  373.7 4.9 custom-call.14
  378.9 57.9 %all_gather.9 = f32[64,2048]{0,1:T(8,128)S(1)} all-gather(f32[64,64]{0,1:T(8,128)S(1)} %copy.80), channel_id=1, replica_groups=mesh['row'=16,'col'=32] {'col'}, dimensions={1}, use_global_device_ids=true | all-gather | bytes 540672 | tf_op jit(solution)/shard_map/all_gather | solution.py:79
  439.9 1.2 copy.134
  441.1 71.8 %reduce-scatter.21.cloned.1.call-done = f32[96,64]{1,0:T(8,128)} async-done(((f32[1536,64]{1,0:T(8,128)}), f32[96,64]{1,0:T(8,128)}) %reduce-scatter.21.cloned.1.call-update) | async-done | bytes 24592
  514.9 113.1 %psum.51 = f32[64,64]{0,1:T(8,128)S(1)} all-reduce(f32[64,64]{0,1:T(8,128)S(1)} %fusion.154), channel_id=1, replica_groups=mesh['row'=16,'col'=32] {'row','col'}, use_global_device_ids=true, to_apply=%region_6.12 | all-reduce | flops 4096 | bytes 32768 | tf_op jit(solution)/shard_map/psum | solution.py:94
  628.1 5.8 cholesky.141
  635.3 4.9 custom-call.15
  640.5 18.9 %all_to_all.15 = f32[16,64,96]{2,1,0:T(8,128)S(1)} all-to-all(f32[16,64,96]{2,1,0:T(8,128)S(1)} %stack.23), channel_id=1, replica_groups=mesh['row'=16,'col'=32] {'row'}, dimensions={0} | all-to-all | bytes 786432 | tf_op jit(solution)/shard_map/all_to_all | solution.py:55
  660.6 2.2 convolution_bitcast_fusion.3
  662.8 1.1 convolution_bitcast_fusion.9
  663.9 1.4 copy.135
  665.3 105.9 %reduce-scatter.23.cloned.1.call-done = f32[64,64]{1,0:T(8,128)} async-done(((f32[2048,64]{1,0:T(8,128)}), f32[64,64]{1,0:T(8,128)}) %reduce-scatter.23.cloned.1.call-update) | async-done | bytes 16400
  773.1 102.0 %psum.52 = f32[64,64]{0,1:T(8,128)S(1)} all-reduce(f32[64,64]{0,1:T(8,128)S(1)} %fusion.155), channel_id=1, replica_groups=mesh['row'=16,'col'=32] {'row','col'}, use_global_device_ids=true, to_apply=%region_8.14 | all-reduce | flops 4096 | bytes 32768 | tf_op jit(solution)/shard_map/psum | solution.py:76
  875.2 5.8 cholesky.152
  882.4 4.9 custom-call.16
  887.6 56.8 %all_gather.10 = f32[64,2048]{0,1:T(8,128)S(1)} all-gather(f32[64,64]{0,1:T(8,128)S(1)} %copy.91), channel_id=1, replica_groups=mesh['row'=16,'col'=32] {'col'}, dimensions={1}, use_global_device_ids=true | all-gather | bytes 540672 | tf_op jit(solution)/shard_map/all_gather | solution.py:79
  946.4 1.1 convolution_bitcast_fusion.8
  947.5 1.2 copy.136
  948.7 69.1 %reduce-scatter.25.cloned.1.call-done = f32[96,64]{1,0:T(8,128)} async-done(((f32[1536,64]{1,0:T(8,128)}), f32[96,64]{1,0:T(8,128)}) %reduce-scatter.25.cloned.1.call-update) | async-done | bytes 24592
  1019.8 113.2 %psum.53 = f32[64,64]{0,1:T(8,128)S(1)} all-reduce(f32[64,64]{0,1:T(8,128)S(1)} %fusion.156), channel_id=1, replica_groups=mesh['row'=16,'col'=32] {'row','col'}, use_global_device_ids=true, to_apply=%region_10.16 | all-reduce | flops 4096 | bytes 32768 | tf_op jit(solution)/shard_map/psum | solution.py:94
  1133.1 5.8 cholesky.163
  1140.3 4.9 custom-call.17
  1145.5 19.1 %all_to_all.16 = f32[16,64,96]{2,1,0:T(8,128)S(1)} all-to-all(f32[16,64,96]{2,1,0:T(8,128)S(1)} %stack.24), channel_id=1, replica_groups=mesh['row'=16,'col'=32] {'row'}, dimensions={0} | all-to-all | bytes 786432 | tf_op jit(solution)/shard_map/all_to_all | solution.py:55
  1165.8 2.2 convolution_bitcast_fusion.1
  1168.0 1.1 convolution_bitcast_fusion.7
  1169.1 1.4 copy.137
  1170.5 105.9 %reduce-scatter.27.cloned.1.call-done = f32[64,64]{1,0:T(8,128)} async-done(((f32[2048,64]{1,0:T(8,128)}), f32[64,64]{1,0:T(8,128)}) %reduce-scatter.27.cloned.1.call-update) | async-done | bytes 16400
  1278.3 101.8 %psum.54 = f32[64,64]{0,1:T(8,128)S(1)} all-reduce(f32[64,64]{0,1:T(8,128)S(1)} %fusion.157), channel_id=1, replica_groups=mesh['row'=16,'col'=32] {'row','col'}, use_global_device_ids=true, to_apply=%region_12.18 | all-reduce | flops 4096 | bytes 32768 | tf_op jit(solution)/shard_map/psum | solution.py:76
  1380.3 5.8 cholesky.174
  1387.5 4.9 custom-call.18
  1393.3 56.3 %all_gather.11 = f32[64,2048]{0,1:T(8,128)S(1)} all-gather(f32[64,64]{0,1:T(8,128)S(1)} %copy.102), channel_id=1, replica_groups=mesh['row'=16,'col'=32] {'col'}, dimensions={1}, use_global_device_ids=true | all-gather | bytes 540672 | tf_op jit(solution)/shard_map/all_gather | solution.py:79
  1451.5 1.1 convolution_bitcast_fusion.6
  1452.6 1.2 copy.138
  1454.5 70.3 %reduce-scatter.29.cloned.1.call-done = f32[96,64]{1,0:T(8,128)} async-done(((f32[1536,64]{1,0:T(8,128)}), f32[96,64]{1,0:T(8,128)}) %reduce-scatter.29.cloned.1.call-update) | async-done | bytes 24592
  1526.7 113.1 %psum.55 = f32[64,64]{0,1:T(8,128)S(1)} all-reduce(f32[64,64]{0,1:T(8,128)S(1)} %fusion.158), channel_id=1, replica_groups=mesh['row'=16,'col'=32] {'row','col'}, use_global_device_ids=true, to_apply=%region_14.20 | all-reduce | flops 4096 | bytes 32768 | tf_op jit(solution)/shard_map/psum | solution.py:94
  1639.9 5.8 cholesky.185
  1647.0 4.9 custom-call.19
  (115 shorter events, 40.2 us)
Async XLA Ops:
  7.2 145.0 %copy-start = (bf16[1,1,32,128,128]{4,3,2,1,0:T(8,128)(2,1)S(1)}, bf16[1,1,32,128,128]{4,3,2,1,0:T(8,128)(2,1)}, u32[]{:S(2)}) copy-start(bf16[1,1,32,128,128]{4,3,2,1,0:T(8,128)(2,1)} %param.15) | copy-start | bytes 3145732
  126.0 6.4 copy-start.1
  133.5 17.4 %all-to-all-start = ((f32[16,64,96]{2,1,0:T(8,128)}), f32[16,64,96]{2,1,0:T(8,128)S(1)}, u32[]{:S(2)}, u32[]{:S(2)}) async-start(f32[16,64,96]{2,1,0:T(8,128)} %stack.22), calls=%async_computation | async-start | bytes 1048576 | tf_op jit(solution)/shard_map/all_to_all | solution.py:55
  137.0 126.5 %reduce-scatter.19.cloned.1.call-start = ((), (), s32[]{:S(2)}) async-start(), calls=%async_computation.9 | async-start | bytes 1081344
  137.7 0.7 copy-start.2
  156.8 356.2 %reduce-scatter.21.cloned.1.call-start = ((), (), s32[]{:S(2)}) async-start(), calls=%async_computation.10 | async-start | bytes 835584
  441.1 330.1 %reduce-scatter.23.cloned.1.call-start = ((), (), s32[]{:S(2)}) async-start(), calls=%async_computation.11 | async-start | bytes 1081344
  665.3 352.6 %reduce-scatter.25.cloned.1.call-start = ((), (), s32[]{:S(2)}) async-start(), calls=%async_computation.12 | async-start | bytes 835584
  948.7 327.7 %reduce-scatter.27.cloned.1.call-start = ((), (), s32[]{:S(2)}) async-start(), calls=%async_computation.13 | async-start | bytes 1081344
  1170.5 354.3 %reduce-scatter.29.cloned.1.call-start = ((), (), s32[]{:S(2)}) async-start(), calls=%async_computation.14 | async-start | bytes 835584
Sparse Core Ops, SparseCore 0:
  156.9 106.6 reduce-scatter.18
  441.2 71.6 reduce-scatter.20
  665.4 105.7 reduce-scatter.22
  948.8 69.0 reduce-scatter.24
  1170.6 105.8 reduce-scatter.26
  1453.9 70.7 reduce-scatter.28
